TPU v7x, 256 devices: a whole 4x4x8 slice. The times are simulated.
256 devices in a mesh: ctx: 8 (over z_lo, core), dp: 8 (over z_hi, y), head: 4 (over x).
Axes of the slice: x: 4, y: 4, z: 8 (z_hi: 2, z_lo: 4; z = z_hi * 4 + z_lo), core: 2. Of those that a mesh axis runs over, the one named last changes fastest.
Arguments:
- queries: bfloat16 [32768, 8, 128], P(('dp', 'ctx'), 'head'), parts along dimension 0, may hold values from -40 to 40
- keys: bfloat16 [32768, 128], P(('dp', 'ctx')), parts along dimension 0, may hold values from -6 to 6
- values: bfloat16 [32768, 128], P(('dp', 'ctx')), parts along dimension 0, may hold values from -6 to 6
- output: bfloat16 [32768, 8, 128], P(('dp', 'ctx'), 'head'), parts along dimension 0, may hold values from -6 to 6
- output_grad: bfloat16 [32768, 8, 128], P(('dp', 'ctx'), 'head'), parts along dimension 0, may hold values from -6 to 6
- block_doc: int32 [256], P('dp'), parts along dimension 0, may hold values from 0 to 3, never falling along the last dimension, each value on 1 to 24 neighbouring positions
Outputs:
- query_grad: bfloat16 [32768, 8, 128], P(('dp', 'ctx'), 'head'), parts along dimension 0
- key_grad: bfloat16 [32768, 128], P(('dp', 'ctx', 'head')), parts along dimension 0
- value_grad: bfloat16 [32768, 128], P(('dp', 'ctx', 'head')), parts along dimension 0
There are 8 independent parts, one for each index of `dp`. A program takes and returns all parts, laid end to end along the dimension named above; each array names one. Nothing has to cross between parts.
Inputs may be any that keep to these rules, and one draw needn't show every extreme that they name: block_doc[b] is the document of tokens b * 128 to (b + 1) * 128 - 1; ids never fall; each of the 4 documents spans 1 to 24 blocks, and one spans exactly 24.
All inputs are finite; a program needn't handle non-finite values.
Results may differ from a plain program's by a relative error of at most 0.0049.
Values may be sent and summed in bfloat16 or wider, within the bound.
No kernel may reach another device: no remote copies, remote signals or barrier semaphores. Data moves between devices by JAX's collectives and lax.ppermute only.
A program may use at most 64 MiB of HBM per device.

v0:
```python
import jax
import jax.numpy as jnp
from jax import lax
from jax.sharding import PartitionSpec as P

BLK = 128
masked_score = -1e30


def local(queries, keys, values, output, output_grad, block_doc):
    shard_rows = queries.shape[0]
    heads_here = queries.shape[1]
    head_size = queries.shape[2]
    cycle_length = lax.axis_size("ctx")
    seq_tokens = shard_rows * cycle_length
    ctx_index = lax.axis_index("ctx")
    inv_root = head_size ** (-0.5)
    doc_tok = jnp.broadcast_to(block_doc[:, None], (block_doc.shape[0], BLK)).reshape(seq_tokens)
    row_ids = jnp.arange(shard_rows, dtype=jnp.int32)

    def positions_of(anchor):
        return anchor * shard_rows + row_ids

    query_pos = positions_of(ctx_index)
    query_doc = jnp.take(doc_tok, query_pos)
    row_delta = jnp.sum(output_grad.astype(jnp.float32) * output.astype(jnp.float32), axis=-1)

    def visible(anchor):
        key_pos = positions_of(anchor)
        key_doc = jnp.take(doc_tok, key_pos)
        return (key_pos[None, :] <= query_pos[:, None]) & (key_doc[None, :] == query_doc[:, None])

    def scores(key_tile, visible_mask):
        score_tile = (
            jnp.einsum("bhd,kd->bhk", queries, key_tile, preferred_element_type=jnp.float32)
            * inv_root
        )
        return jnp.where(visible_mask[:, None, :], score_tile, masked_score)

    def stat_step(stats_pair, key_tile, anchor):
        visible_mask = visible(anchor)
        running_max, running_sum = stats_pair
        score_tile = scores(key_tile, visible_mask)
        new_max = jnp.maximum(running_max, jnp.max(score_tile, axis=-1))
        terms = jnp.where(visible_mask[:, None, :], jnp.exp(score_tile - new_max[..., None]), 0.0)
        return (new_max, running_sum * jnp.exp(running_max - new_max) + jnp.sum(terms, axis=-1))

    def grad_step(key_tile, value_tile, anchor, log_total):
        visible_mask = visible(anchor)
        score_tile = scores(key_tile, visible_mask)
        prob = jnp.where(visible_mask[:, None, :], jnp.exp(score_tile - log_total[..., None]), 0.0)
        prob_low = prob.astype(jnp.bfloat16)
        prob_grad = jnp.einsum(
            "bhd,kd->bhk", output_grad, value_tile, preferred_element_type=jnp.float32
        )
        score_grad = (prob * (prob_grad - row_delta[..., None])).astype(jnp.bfloat16)
        query_part = (
            jnp.einsum("bhk,kd->bhd", score_grad, key_tile, preferred_element_type=jnp.float32)
            * inv_root
        )
        key_part = (
            jnp.einsum("bhk,bhd->kd", score_grad, queries, preferred_element_type=jnp.float32)
            * inv_root
        )
        value_part = jnp.einsum(
            "bhk,bhd->kd", prob_low, output_grad, preferred_element_type=jnp.float32
        )
        return (query_part, jnp.stack([key_part, value_part], axis=1))

    stats_start = (
        jnp.full((shard_rows, heads_here), masked_score, jnp.float32),
        jnp.zeros((shard_rows, heads_here), jnp.float32),
    )
    query_start = jnp.zeros((shard_rows, heads_here, head_size), jnp.float32)
    key_all, value_all = (
        lax.all_gather(keys, "ctx", axis=0, tiled=True),
        lax.all_gather(values, "ctx", axis=0, tiled=True),
    )

    def stat_loop(step_index, stats_pair):
        key_tile = lax.dynamic_slice_in_dim(key_all, step_index * shard_rows, shard_rows, 0)
        return stat_step(stats_pair, key_tile, step_index)

    running_max, running_sum = lax.fori_loop(0, cycle_length, stat_loop, stats_start)
    log_total = running_max + jnp.log(running_sum)

    def grad_loop(query_acc, step_index):
        key_tile = lax.dynamic_slice_in_dim(key_all, step_index * shard_rows, shard_rows, 0)
        value_tile = lax.dynamic_slice_in_dim(value_all, step_index * shard_rows, shard_rows, 0)
        query_part, pair_part = grad_step(key_tile, value_tile, step_index, log_total)
        return (query_acc + query_part, pair_part)

    query_acc, pair_blocks = lax.scan(
        grad_loop, query_start, jnp.arange(cycle_length, dtype=jnp.int32)
    )
    partial_grads = pair_blocks.reshape(seq_tokens, 2, head_size)
    owned_rows = lax.psum_scatter(partial_grads, ("ctx", "head"), scatter_dimension=0, tiled=True)
    query_grad = query_acc.astype(jnp.bfloat16)
    key_grad = owned_rows[:, 0, :].astype(jnp.bfloat16)
    value_grad = owned_rows[:, 1, :].astype(jnp.bfloat16)
    return (query_grad, key_grad, value_grad)


def solution(mesh):
    placed = (
        P(("dp", "ctx"), "head", None),
        P(("dp", "ctx"), None),
        P(("dp", "ctx"), None),
        P(("dp", "ctx"), "head", None),
        P(("dp", "ctx"), "head", None),
        P("dp"),
    )
    return jax.shard_map(
        local,
        mesh=mesh,
        in_specs=placed,
        out_specs=(
            P(("dp", "ctx"), "head", None),
            P(("dp", "ctx", "head"), None),
            P(("dp", "ctx", "head"), None),
        ),
        check_vma=False,
    )
```

profile of v0, /device:TPU:24, one launch (start us, length us, event | category | flops | bytes accessed | tf_op | source)
XLA Modules:
  0.0 344.0 jit_solution(15952463932650075983)
XLA Ops:
  9.5 3.1 gather_fusion.2
  13.6 36.0 %all-gather.3.cloned.1.call-done = bf16[4096,128]{1,0:T(8,128)(2,1)} async-done(((bf16[512,128]{1,0:T(8,128)(2,1)}), bf16[4096,128]{1,0:T(8,128)(2,1)}) %all-gather.3.cloned.1.call-update) | async-done | bytes 1048592 | tf_op jit(solution)/shard_map/all_gather | solution.py:76
  49.6 45.2 %while.29 = (s32[]{:T(128)}, f32[512,2]{0,1:T(2,128)S(1)}, f32[512,2]{0,1:T(2,128)S(1)}, s32[512]{0:T(512)S(1)}, bf16[4096,128]{1,0:T(8,128)(2,1)}, /*index=5*/b...) while((s32[]{:T(128)}, f32[512,2]{0,1:T(2,128)S(1)}, ...), condition=%wide.region_3.5_spmd.clone, body=%wide.region_0.4_spmd.clone.sunk | while | flops 139211264 | bytes 5474630 | solution.py:84
  49.7 3.1 gather_fusion
  55.4 3.1 gather_fusion
  61.0 3.1 gather_fusion
  66.7 3.1 gather_fusion
  72.3 3.1 gather_fusion
  78.0 3.1 gather_fusion
  83.6 3.1 gather_fusion
  89.3 3.1 gather_fusion
  94.8 89.5 %while.30 = (s32[]{:T(128)}, f32[512,2,128]{2,0,1:T(8,128)S(1)}, f32[8,512,2,128]{3,1,0,2:T(8,128)}, s32[8]{0:T(128)S(1)}, s32[512]{0:T(512)S(1)}, /*index=5*/bf...) while((s32[]{:T(128)}, f32[512,2,128]{2,0,1:T(8,128)S(1)}, ...), condition=%wide.region_6.8_spmd.clone, body=%wide.region_5.7_spmd.clone.sunk | while | flops 676666880 | bytes 14080389 | solution.py:93
  96.2 3.1 gather_fusion.1
  99.7 1.7 fusion.77
  107.4 3.1 gather_fusion.1
  110.9 1.7 fusion.77
  114.8 1.6 fusion.79
  118.6 3.1 gather_fusion.1
  122.0 1.7 fusion.77
  129.8 3.1 gather_fusion.1
  133.2 1.7 fusion.77
  141.0 3.1 gather_fusion.1
  144.4 1.7 fusion.77
  152.1 3.1 gather_fusion.1
  155.6 1.7 fusion.77
  159.5 1.6 fusion.79
  163.3 3.1 gather_fusion.1
  166.8 1.7 fusion.77
  170.7 1.6 fusion.79
  174.5 3.1 gather_fusion.1
  177.9 1.7 fusion.77
  185.5 150.5 %reduce-scatter.2.cloned.1.call-done = f32[128,2,128]{2,0,1:T(8,128)} async-done(((f32[4096,2,128]{2,0,1:T(8,128)}), f32[128,2,128]{2,0,1:T(8,128)}) %reduce-scatter.2.cloned.1.call-update) | async-done | bytes 131088 | tf_op jit(solution)/shard_map/reduce_scatter | solution.py:97
  (213 shorter events, 65.5 us)
Async XLA Ops:
  7.2 5.5 %copy-start.2 = (bf16[512,2,128]{2,1,0:T(2,128)(2,1)S(1)}, bf16[512,2,128]{2,1,0:T(2,128)(2,1)}, u32[]{:S(2)}) copy-start(bf16[512,2,128]{2,1,0:T(2,128)(2,1)} %param.12) | copy-start | bytes 786436
  7.2 5.6 %copy-start = (bf16[512,2,128]{2,1,0:T(2,128)(2,1)S(1)}, bf16[512,2,128]{2,1,0:T(2,128)(2,1)}, u32[]{:S(2)}) copy-start(bf16[512,2,128]{2,1,0:T(2,128)(2,1)} %param.16) | copy-start | bytes 786436
  7.2 5.6 %copy-start.1 = (bf16[512,2,128]{2,1,0:T(2,128)(2,1)S(1)}, bf16[512,2,128]{2,1,0:T(2,128)(2,1)}, u32[]{:S(2)}) copy-start(bf16[512,2,128]{2,1,0:T(2,128)(2,1)} %param.15) | copy-start | bytes 786436
  7.2 42.4 %all-gather.3.cloned.1.call-start = ((), (), s32[]{:S(2)}) async-start(), calls=%async_computation.1 | async-start | bytes 1179648 | tf_op jit(solution)/shard_map/all_gather | solution.py:76
  7.9 86.9 %all-gather.5.cloned.1.call-start = ((), (), s32[]{:S(2)}) async-start(), calls=%async_computation.2 | async-start | bytes 1179648 | tf_op jit(solution)/shard_map/all_gather | solution.py:77
  8.7 327.3 %reduce-scatter.2.cloned.1.call-start = ((), (), s32[]{:S(2)}) async-start(), calls=%async_computation.3 | async-start | bytes 4325376 | tf_op jit(solution)/shard_map/reduce_scatter | solution.py:97
  9.5 40.1 %copy-start.3 = (s32[32]{0:T(128)S(1)}, s32[32]{0:T(128)}, u32[]{:S(2)}) copy-start(s32[32]{0:T(128)} %param.17) | copy-start | bytes 388
Sparse Core Ops, SparseCore 0:
  9.8 39.7 all-gather.2
  51.4 35.9 all-gather.4
  184.5 151.4 reduce-scatter.1
where the time goes:
time: 345 us; the launch traced here: 344 us
  waiting for transfers between devices  188 us (54%)
  local copies, waits for them, and re-layouts  61.8 us (18%)
  matrix products  55.9 us (16%)
  other arithmetic  17.8 us (5%)
  between operations  13.9 us (4%)
  loops' own time  6.6 us (2%)
    reduce_scatter x1, waiting for transfers between devices, local(): lax.psum_scatter(partial_grads, ('ctx', 'head'), scatter_dimension=0, til...  150 us
    gather x16, local copies, waits for them, and re-layouts, visible(): key_doc = jnp.take(doc_tok, key_pos)  50.2 us
    all_gather x1, waiting for transfers between devices, local(): lax.all_gather(keys, 'ctx', axis=0, tiled=True)  36 us
    dot_general x16, matrix products, scores(): jnp.einsum('bhd,kd->bhk', queries, key_tile, preferred_element_type=jnp.f...  25.1 us
    dot_general x8, matrix products, grad_step(): jnp.einsum('bhk,kd->bhd', score_grad, key_tile, preferred_element_type=jn...  12.8 us
    dot_general x8, matrix products, grad_step(): jnp.einsum('bhd,kd->bhk', output_grad, value_tile, preferred_element_type...  10.8 us
  transfers between devices with their start and end apart: 3, of which 2 were waited for; matrix products, arithmetic and copies ran while one was open for 15% of the time, Pallas kernels for 0%

commit v1 on v0

--- a/solution.py
+++ b/solution.py
@@ -73,7 +73,9 @@
     )
     query_start = jnp.zeros((shard_rows, heads_here, head_size), jnp.float32)
     key_all, value_all = (
-        lax.all_gather(keys, "ctx", axis=0, tiled=True),
+        jnp.concatenate(
+            lax.all_to_all(jnp.stack([keys] * lax.axis_size("ctx")), "ctx", 0, 0), axis=0
+        ),
         lax.all_gather(values, "ctx", axis=0, tiled=True),
     )
 

time: 345 us -> 322 us (0.933)
  matrix products: 55.9 us -> 33.9 us
  waiting for transfers between devices: 188 us -> 179 us
  starting transfers between devices: 0.11 us -> 6.11 us
    all_gather x1 -> x0, waiting for transfers between devices: 36 us -> none  [local(): lax.all_gather(keys, 'ctx', axis=0, tiled=True)]
    all_to_all x0 -> x1, waiting for transfers between devices: none -> 27 us  [local(): lax.all_to_all(jnp.stack([keys] * lax.axis_size('ctx')), 'ctx', 0, 0)]
    dot_general x16, matrix products: 25.1 us -> 10.7 us  [scores(): jnp.einsum('bhd,kd->bhk', queries, key_tile, preferred_element_type=jnp.f...]
    dot_general x8, matrix products: 12.8 us -> 5.45 us  [grad_step(): jnp.einsum('bhk,kd->bhd', score_grad, key_tile, preferred_element_type=jn...]
    all_to_all x0 -> x1, starting transfers between devices: none -> 6.03 us  [local(): lax.all_to_all(jnp.stack([keys] * lax.axis_size('ctx')), 'ctx', 0, 0)]
  transfers between devices with their start and end apart: 3 -> 3, of which waited for: 2 -> 2; matrix products, arithmetic and copies ran while one was open for 15% -> 13% of each run, Pallas kernels for 0% -> 0%
where the time goes in v1:
time: 322 us; the launch traced here: 321 us
  waiting for transfers between devices  179 us (56%)
  local copies, waits for them, and re-layouts  63.2 us (20%)
  matrix products  33.9 us (11%)
  other arithmetic  17.8 us (6%)
  between operations  14.2 us (4%)
  loops' own time  6.59 us (2%)
  starting transfers between devices  6.11 us (2%)
    reduce_scatter x1, waiting for transfers between devices, local(): lax.psum_scatter(partial_grads, ('ctx', 'head'), scatter_dimension=0, til...  152 us
    gather x16, local copies, waits for them, and re-layouts, visible(): key_doc = jnp.take(doc_tok, key_pos)  50.2 us
    all_to_all x1, waiting for transfers between devices, local(): lax.all_to_all(jnp.stack([keys] * lax.axis_size('ctx')), 'ctx', 0, 0)  27 us
    dot_general x8, matrix products, grad_step(): jnp.einsum('bhd,kd->bhk', output_grad, value_tile, preferred_element_type...  10.8 us
    dot_general x16, matrix products, scores(): jnp.einsum('bhd,kd->bhk', queries, key_tile, preferred_element_type=jnp.f...  10.7 us
    dynamic_update_slice x8, other arithmetic, local(): lax.scan(grad_loop, query_start, jnp.arange(cycle_length, dtype=jnp.int32))  6.73 us
  transfers between devices with their start and end apart: 3, of which 2 were waited for; matrix products, arithmetic and copies ran while one was open for 13% of the time, Pallas kernels for 0%

profile of v1, /device:TPU:24, one launch (start us, length us, event | category | flops | bytes accessed | tf_op | source)
XLA Modules:
  0.0 321.2 jit_solution(989101603923442751)
XLA Ops:
  7.2 2.1 stack.8
  9.3 6.0 %all-to-all-start = ((bf16[8,512,128]{2,1,0:T(8,128)(2,1)}), bf16[8,512,128]{2,1,0:T(8,128)(2,1)S(1)}, u32[]{:S(2)}, u32[]{:S(2)}) async-start(bf16[8,512,128]{2,1,0:T(8,128)(2,1)} %stack.8), calls=%async_computation | async-start | bytes 2097152 | tf_op jit(solution)/shard_map/all_to_all | solution.py:77
  17.2 3.1 gather_fusion.2
  20.3 27.0 %all-to-all-done = bf16[8,512,128]{2,1,0:T(8,128)(2,1)S(1)} async-done(((bf16[8,512,128]{2,1,0:T(8,128)(2,1)}), bf16[8,512,128]{2,1,0:T(8,128)(2,1)S(1)}, u32[]{:S(2)}, u32[]{:S(2)}) %all-to-all-start) | async-done | bytes 1048608 | tf_op jit(solution)/shard_map/all_to_all | solution.py:77
  47.3 37.9 %while.29 = (s32[]{:T(128)}, f32[512,2]{0,1:T(2,128)S(1)}, f32[512,2]{0,1:T(2,128)S(1)}, s32[512]{0:T(512)S(1)}, bf16[4096,128]{1,0:T(8,128)(2,1)S(1)}, /*index=...) while((s32[]{:T(128)}, f32[512,2]{0,1:T(2,128)S(1)}, ...), condition=%wide.region_3.5_spmd.clone, body=%wide.region_0.4_spmd.clone.sunk | while | flops 139211264 | bytes 5474630 | solution.py:86
  47.4 3.1 gather_fusion
  52.2 3.1 gather_fusion
  56.9 3.1 gather_fusion
  61.6 3.1 gather_fusion
  66.4 3.1 gather_fusion
  71.1 3.1 gather_fusion
  75.9 3.1 gather_fusion
  80.6 3.1 gather_fusion
  85.3 74.8 %while.30 = (s32[]{:T(128)}, f32[512,2,128]{2,0,1:T(8,128)S(1)}, f32[8,512,2,128]{3,1,0,2:T(8,128)}, s32[8]{0:T(128)S(1)}, s32[512]{0:T(512)S(1)}, /*index=5*/bf...) while((s32[]{:T(128)}, f32[512,2,128]{2,0,1:T(8,128)S(1)}, ...), condition=%wide.region_6.8_spmd.clone, body=%wide.region_5.7_spmd.clone.sunk | while | flops 676666880 | bytes 14080389 | solution.py:95
  86.6 3.1 gather_fusion.1
  91.3 1.3 fusion.78
  96.0 3.1 gather_fusion.1
  100.7 1.3 fusion.78
  105.3 3.1 gather_fusion.1
  110.0 1.3 fusion.78
  114.7 3.1 gather_fusion.1
  119.4 1.3 fusion.78
  124.1 3.1 gather_fusion.1
  128.7 1.3 fusion.78
  133.4 3.1 gather_fusion.1
  138.1 1.3 fusion.78
  142.8 3.1 gather_fusion.1
  147.4 1.3 fusion.78
  152.1 3.1 gather_fusion.1
  156.8 1.3 fusion.78
  160.1 1.1 copy.33
  161.2 151.6 %reduce-scatter.2.cloned.1.call-done = f32[128,2,128]{2,0,1:T(8,128)} async-done(((f32[4096,2,128]{2,0,1:T(8,128)}), f32[128,2,128]{2,0,1:T(8,128)}) %reduce-scatter.2.cloned.1.call-update) | async-done | bytes 131088 | tf_op jit(solution)/shard_map/reduce_scatter | solution.py:99
  (213 shorter events, 48.5 us)
Async XLA Ops:
  7.2 9.0 %copy-start.2 = (bf16[512,2,128]{2,1,0:T(2,128)(2,1)S(1)}, bf16[512,2,128]{2,1,0:T(2,128)(2,1)}, u32[]{:S(2)}) copy-start(bf16[512,2,128]{2,1,0:T(2,128)(2,1)} %param.12) | copy-start | bytes 786436
  7.2 9.0 %copy-start = (bf16[512,2,128]{2,1,0:T(2,128)(2,1)S(1)}, bf16[512,2,128]{2,1,0:T(2,128)(2,1)}, u32[]{:S(2)}) copy-start(bf16[512,2,128]{2,1,0:T(2,128)(2,1)} %param.16) | copy-start | bytes 786436
  7.2 9.1 %copy-start.1 = (bf16[512,2,128]{2,1,0:T(2,128)(2,1)S(1)}, bf16[512,2,128]{2,1,0:T(2,128)(2,1)}, u32[]{:S(2)}) copy-start(bf16[512,2,128]{2,1,0:T(2,128)(2,1)} %param.15) | copy-start | bytes 786436
  9.3 7.8 %copy-start.3 = (s32[32]{0:T(128)S(1)}, s32[32]{0:T(128)}, u32[]{:S(2)}) copy-start(s32[32]{0:T(128)} %param.17) | copy-start | bytes 388
  9.3 38.0 %all-to-all-start = ((bf16[8,512,128]{2,1,0:T(8,128)(2,1)}), bf16[8,512,128]{2,1,0:T(8,128)(2,1)S(1)}, u32[]{:S(2)}, u32[]{:S(2)}) async-start(bf16[8,512,128]{2,1,0:T(8,128)(2,1)} %stack.8), calls=%async_computation | async-start | bytes 2097152 | tf_op jit(solution)/shard_map/all_to_all | solution.py:77
  15.3 69.9 %all-gather.2.cloned.1.call-start = ((), (), s32[]{:S(2)}) async-start(), calls=%async_computation.2 | async-start | bytes 1179648 | tf_op jit(solution)/shard_map/all_gather | solution.py:79
  16.1 296.8 %reduce-scatter.2.cloned.1.call-start = ((), (), s32[]{:S(2)}) async-start(), calls=%async_computation.3 | async-start | bytes 4325376 | tf_op jit(solution)/shard_map/reduce_scatter | solution.py:99
Sparse Core Ops, SparseCore 0:
  17.9 38.6 all-gather.1
  160.2 152.5 reduce-scatter.1
